TPU v7x, 256 devices: a whole 4x4x8 slice. The times are simulated.
256 devices in a mesh: dom: 32 (over y, z_hi, x), cls: 8 (over z_lo, core).
Axes of the slice: x: 4, y: 4, z: 8 (z_hi: 2, z_lo: 4; z = z_hi * 4 + z_lo), core: 2. Of those that a mesh axis runs over, the one named last changes fastest.
Arguments:
- spectra: bfloat16 [32768, 2, 16512], P('dom', None, 'cls'), may hold values from -6 to 6
- classes: int32 [32768], P('dom'), may hold values from 0 to 63
- halves: int32 [32768], P('dom'), may hold values from 0 to 1
- groups: int32 [32768], P('dom'), may hold values from 0 to 15
- cycles: int32 [16512], P('dom'), may hold values from 0 to 127
- ctf_table: bfloat16 [16, 16512], replicated, may hold values from -1 to 1
- noise: float32 [128], replicated, may hold values from 0.5 to 8
Outputs:
- averages: bfloat16 [64, 2, 16512], replicated
All inputs are finite; a program needn't handle non-finite values.
Results may differ from a plain program's by a relative error of at most 0.0067.
Values may be sent and summed in bfloat16 or wider, within the bound.
A program may use at most 64 MiB of HBM per device.

v0:
```python
import jax
import jax.numpy as jnp
from jax import lax
from jax.sharding import PartitionSpec as P

K = 64


RIDGE = 1.0
GAIN_FLOOR = 0.02
EPSILON = 1e-06


def to_owners(partial_sums):
    return lax.all_to_all(partial_sums, "cls", split_axis=1, concat_axis=3, tiled=True)


def local(spectra, classes, halves, groups, cycles, ctf_table, noise):
    highest = lax.Precision.HIGHEST
    local_pixels = spectra.shape[2]
    depth = ctf_table.shape[0]
    pixels = ctf_table.shape[1]
    cycle_total = noise.shape[0]
    dom_count = lax.axis_size("dom")
    pixel_share = pixels // dom_count
    square_table = (ctf_table.astype(jnp.float32) ** 2).astype(jnp.bfloat16)
    pixel_begin = lax.axis_index("cls") * local_pixels
    ctf_local = lax.dynamic_slice_in_dim(ctf_table, pixel_begin, local_pixels, 1)
    group_hot = (groups[:, None] == jnp.arange(depth, dtype=jnp.int32)[None, :]).astype(
        jnp.bfloat16
    )
    labels = halves * K + classes
    class_hot = (labels[:, None] == jnp.arange(2 * K, dtype=jnp.int32)[None, :]).astype(
        jnp.bfloat16
    )
    ctf = jnp.dot(group_hot, ctf_local, preferred_element_type=jnp.float32)
    weighted = (ctf[:, None, :] * spectra).astype(jnp.bfloat16)
    square_local = lax.dynamic_slice_in_dim(square_table, pixel_begin, local_pixels, 1)
    squares = jnp.dot(group_hot, square_local, preferred_element_type=jnp.float32).astype(
        jnp.bfloat16
    )
    stacked = jnp.concatenate([weighted, squares[:, None, :]], axis=1)
    channels = stacked.shape[1]
    partial_sums = jnp.einsum("pm,pcn->mcn", class_hot, stacked, preferred_element_type=jnp.float32)
    partial_sums = partial_sums.reshape(2, K, channels, local_pixels)
    summed = lax.psum(partial_sums, "dom")
    owned = to_owners(summed)
    owned = lax.dynamic_slice_in_dim(owned, lax.axis_index("dom") * pixel_share, pixel_share, 3)
    owned = jnp.transpose(owned, (1, 0, 2, 3))
    sums = owned[:, :, 0:2, :]
    wsum = owned[:, :, 2, :]
    halfavg = sums / (wsum[:, :, None, :] + RIDGE)
    first_half = halfavg[:, 0]
    second_half = halfavg[:, 1]
    merged = (sums[:, 0] + sums[:, 1]) / (wsum[:, 0] + wsum[:, 1] + RIDGE)[:, None, :]
    cross = jnp.sum(first_half * second_half, axis=1)
    power_zero = jnp.sum(first_half * first_half, axis=1)
    power_one = jnp.sum(second_half * second_half, axis=1)
    statistics = jnp.stack([cross, power_zero, power_one], axis=1)
    cycle_hot = (cycles[:, None] == jnp.arange(cycle_total, dtype=jnp.int32)[None, :]).astype(
        jnp.float32
    )
    cycle_local = jnp.einsum("ksn,nr->ksr", statistics, cycle_hot, precision=highest)
    cycle_totals = lax.psum(cycle_local, "dom")
    correlation = cycle_totals[:, 0] / jnp.sqrt(
        (cycle_totals[:, 1] + noise[None, :]) * (cycle_totals[:, 2] + noise[None, :])
    )
    gain = jnp.maximum(correlation, GAIN_FLOOR)
    gain_pixels = jnp.dot(gain, cycle_hot.T, precision=highest)
    filtered = merged * gain_pixels[:, None, :]
    power_total = lax.psum(jnp.sum(filtered * filtered, axis=(1, 2)), "dom")
    power_mean = power_total / (2.0 * pixels)
    normalized = (filtered / jnp.sqrt(power_mean + EPSILON)[:, None, None]).astype(jnp.bfloat16)
    every_class = lax.all_gather(normalized, "cls", axis=0, tiled=True)
    return lax.all_gather(every_class, "dom", axis=2, tiled=True)


def solution(mesh):
    placed = (P("dom", None, "cls"), P("dom"), P("dom"), P("dom"), P("dom"), P(), P())
    return jax.shard_map(local, mesh=mesh, in_specs=placed, out_specs=P(), check_vma=False)
```

profile of v0, /device:TPU:25, one launch (start us, length us, event | category | flops | bytes accessed | tf_op | source)
XLA Modules:
  0.0 1077.0 jit_solution(9439198371304088672)
XLA Ops:
  6.5 0.0 all-reduce.2.cloned.1.call-start
  6.5 2.5 fusion.5
  9.0 2.3 fusion.4
  11.4 0.0 copy-done
  11.4 0.0 copy-start.2
  11.4 0.0 copy-start.3
  11.4 3.1 multiply_convert_fusion
  14.5 0.0 copy-done.2
  14.5 0.0 copy-done.3
  14.5 6.8 fusion
  21.3 0.0 all-reduce.2.cloned.1.call-update
  21.4 407.8 %all-reduce.2.cloned.1.call-done = f32[2,64,3,2064]{3,1,0,2:T(8,128)} async-done(((f32[2,64,3,2064]{3,1,0,2:T(8,128)}), f32[2,64,3,2064]{3,1,0,2:T(8,128)}) %all-reduce.2.cloned.1.call-update) | async-done | bytes 3170320 | tf_op jit(solution)/shard_map/psum | solution.py:46
  429.1 6.3 copy.14
  435.4 23.9 %all-to-all-start = ((f32[2,64,3,2064]{3,0,2,1:T(2,128)}), f32[2,64,3,2064]{3,0,2,1:T(2,128)S(1)}, u32[]{:S(2)}, u32[]{:S(2)}) async-start(f32[2,64,3,2064]{3,0,2,1:T(2,128)} %copy.14), calls=%async_computation | async-start | bytes 6684672 | tf_op jit(solution)/shard_map/all_to_all | solution.py:15
  459.3 74.9 %all-to-all-done = f32[2,64,3,2064]{3,0,2,1:T(2,128)S(1)} async-done(((f32[2,64,3,2064]{3,0,2,1:T(2,128)}), f32[2,64,3,2064]{3,0,2,1:T(2,128)S(1)}, u32[]{:S(2)}, u32[]{:S(2)}) %all-to-all-start) | async-done | bytes 3170336 | tf_op jit(solution)/shard_map/all_to_all | solution.py:15
  534.2 0.2 copy.21
  534.4 0.0 copy-start.4
  534.4 0.0 copy-start.5
  534.4 0.6 copy.16
  535.0 2.7 all_to_all.16
  537.7 1.0 dynamic-slice_bitcast_fusion
  538.8 0.3 fusion.10
  539.1 184.4 %psum.22 = f32[8,3,128]{2,0,1:T(8,128)S(1)} all-reduce(f32[8,3,128]{2,0,1:T(8,128)S(1)} %fusion.10), channel_id=1, replica_groups=mesh['dom'=32,'cls'=8] {'dom'}, use_global_device_ids=true, to_apply=%region_4.0 | all-reduce | flops 3072 | bytes 24576 | tf_op jit(solution)/shard_map/psum | solution.py:64
  723.5 0.3 fusion.8
  723.8 0.1 multiply_reduce_fusion
  723.9 95.3 %psum.23 = f32[8]{0:T(128)S(1)} all-reduce(f32[8]{0:T(128)S(1)} %get-tuple-element.8), channel_id=1, replica_groups=mesh['dom'=32,'cls'=8] {'dom'}, use_global_device_ids=true, to_apply=%region_6.0 | all-reduce | flops 8 | bytes 64 | tf_op jit(solution)/shard_map/psum | solution.py:71
  819.3 0.1 divide_convert_fusion
  819.3 56.2 %all_gather.6 = bf16[64,2,516]{2,0,1:T(8,128)(2,1)S(1)} all-gather(bf16[8,2,516]{2,0,1:T(8,128)(2,1)S(1)} %divide_convert_fusion), channel_id=1, replica_groups=mesh['dom'=32,'cls'=8] {'cls'}, dimensions={0}, use_global_device_ids=true | all-gather | bytes 148608 | tf_op jit(solution)/shard_map/all_gather | solution.py:74
  875.6 0.9 copy.17
  876.5 0.0 all-gather.2.cloned.1.call-update
  876.5 172.1 %all-gather.2.cloned.1.call-done = bf16[64,2,16512]{0,1,2:T(2,128)(2,1)} async-done(((bf16[64,2,516]{0,1,2:T(2,128)(2,1)}), bf16[64,2,16512]{0,1,2:T(2,128)(2,1)}) %all-gather.2.cloned.1.call-update) | async-done | bytes 4227088 | tf_op jit(solution)/shard_map/all_gather | solution.py:75
  1048.6 21.6 %copy.18 = bf16[64,2,16512]{2,1,0:T(2,128)(2,1)} copy(bf16[64,2,16512]{0,1,2:T(2,128)(2,1)} %all-gather.2.cloned.1.call-done) | data formatting | bytes 8454144 | tf_op jit(solution)/shard_map/all_gather | solution.py:75
  (12 shorter events, 0.1 us)
Async XLA Ops:
  6.5 2.5 copy-start.1
  6.5 422.6 %all-reduce.2.cloned.1.call-start = ((), (), s32[]{:S(2)}) async-start(), calls=%async_computation.1 | async-start | bytes 6684672 | tf_op jit(solution)/shard_map/psum | solution.py:46
  6.5 4.8 copy-start
  11.4 3.1 copy-start.2
  11.4 3.1 copy-start.3
  435.4 98.8 %all-to-all-start = ((f32[2,64,3,2064]{3,0,2,1:T(2,128)}), f32[2,64,3,2064]{3,0,2,1:T(2,128)S(1)}, u32[]{:S(2)}, u32[]{:S(2)}) async-start(f32[2,64,3,2064]{3,0,2,1:T(2,128)} %copy.14), calls=%async_computation | async-start | bytes 6684672 | tf_op jit(solution)/shard_map/all_to_all | solution.py:15
  459.3 589.3 %all-gather.2.cloned.1.call-start = ((), (), s32[]{:S(2)}) async-start(), calls=%async_computation.2 | async-start | bytes 8718336 | tf_op jit(solution)/shard_map/all_gather | solution.py:75
  534.4 4.3 copy-start.4
  534.4 189.0 %copy-start.5 = (f32[128]{0:T(128)S(1)}, f32[128]{0:T(128)}, u32[]{:S(2)}) copy-start(f32[128]{0:T(128)} %param.13) | copy-start | bytes 1540
Sparse Core Ops, SparseCore 0:
  21.5 407.6 all-reduce.1
  876.6 171.9 all-gather.1
where the time goes:
time: 1080 us
  waiting for transfers between devices  655 us (61%)
  blocking collectives  336 us (31%)
  local copies, waits for them, and re-layouts  33.3 us (3%)
  starting transfers between devices  23.9 us (2%)
  between operations  13.6 us (1%)
  matrix products  12.2 us (1%)
    psum x1, waiting for transfers between devices, local(): summed = lax.psum(partial_sums, 'dom')  408 us
    psum x1, blocking collectives, local(): cycle_totals = lax.psum(cycle_local, 'dom')  184 us
    all_gather x1, waiting for transfers between devices, local(): return lax.all_gather(every_class, 'dom', axis=2, tiled=True)  172 us
    psum x1, blocking collectives, local(): power_total = lax.psum(jnp.sum(filtered * filtered, axis=(1, 2)), 'dom')  95.3 us
    all_to_all x1, waiting for transfers between devices, to_owners(): lax.all_to_all(partial_sums, 'cls', split_axis=1, concat_axis=3, tiled=True)  74.9 us
    all_gather x1, blocking collectives, local(): every_class = lax.all_gather(normalized, 'cls', axis=0, tiled=True)  56.2 us
    all_to_all x1, starting transfers between devices, to_owners(): lax.all_to_all(partial_sums, 'cls', split_axis=1, concat_axis=3, tiled=True)  23.9 us
    all_gather x1, local copies, waits for them, and re-layouts, local(): return lax.all_gather(every_class, 'dom', axis=2, tiled=True)  21.6 us
  transfers between devices with their start and end apart: 3, of which 3 were waited for; matrix products, arithmetic and copies ran while one was open for 0% of the time, Pallas kernels for 0%

commit v1 on v0

v1 whole, which is shorter than its diff:
```python
import jax
import jax.numpy as jnp
from jax import lax
from jax.sharding import PartitionSpec as P

K = 64
RIDGE = 1.0
GAIN_FLOOR = 0.02
EPSILON = 1e-06
STEP = 32


def local(spectra, classes, halves, groups, cycles, ctf_table, noise):
    highest = lax.Precision.HIGHEST
    local_particles, channels, local_pixels = spectra.shape
    depth = ctf_table.shape[0]
    pixels = ctf_table.shape[1]
    cycle_total = noise.shape[0]
    dom_count = lax.axis_size("dom")
    owned_rows = 2 * K // dom_count
    width = channels * local_pixels
    pixel_begin = lax.axis_index("cls") * local_pixels
    every_cycle = lax.all_gather(cycles, "dom", axis=0, tiled=True)
    ctf_local = lax.dynamic_slice_in_dim(ctf_table, pixel_begin, local_pixels, 1)
    group_hot = (groups[:, None] == jnp.arange(depth, dtype=jnp.int32)[None, :]).astype(
        jnp.bfloat16
    )
    labels = classes * 2 + halves
    class_hot = (labels[:, None] == jnp.arange(2 * K, dtype=jnp.int32)[None, :]).astype(
        jnp.bfloat16
    )
    ctf = jnp.dot(group_hot, ctf_local, preferred_element_type=jnp.float32)
    weighted = (ctf[:, None, :] * spectra).astype(jnp.bfloat16)
    partial_sums = jnp.einsum("pm,pcn->mcn", class_hot, weighted, preferred_element_type=jnp.float32)
    counts = jnp.einsum("pm,pg->mg", class_hot, group_hot, preferred_element_type=jnp.float32)
    high = jnp.floor(counts / STEP)
    low = counts - high * STEP
    message = jnp.concatenate(
        [partial_sums.reshape(2 * K, width), high, low], axis=1
    ).astype(jnp.bfloat16)
    received = lax.all_to_all(
        message.reshape(dom_count, owned_rows, -1), "dom", split_axis=0, concat_axis=0, tiled=True
    )
    total = jnp.sum(received.astype(jnp.float32), axis=0)
    sums = total[:, :width].reshape(owned_rows // 2, 2, channels, local_pixels)
    count_total = total[:, width : width + depth] * STEP + total[:, width + depth :]
    square_local = (ctf_local.astype(jnp.float32) ** 2).astype(jnp.bfloat16).astype(jnp.float32)
    wsum = jnp.dot(count_total, square_local, precision=highest).reshape(
        owned_rows // 2, 2, local_pixels
    )
    halfavg = sums / (wsum[:, :, None, :] + RIDGE)
    first_half = halfavg[:, 0]
    second_half = halfavg[:, 1]
    merged = (sums[:, 0] + sums[:, 1]) / (wsum[:, 0] + wsum[:, 1] + RIDGE)[:, None, :]
    cross = jnp.sum(first_half * second_half, axis=1)
    power_zero = jnp.sum(first_half * first_half, axis=1)
    power_one = jnp.sum(second_half * second_half, axis=1)
    statistics = jnp.stack([cross, power_zero, power_one], axis=1)
    cycle_local = lax.dynamic_slice_in_dim(every_cycle, pixel_begin, local_pixels, 0)
    cycle_hot = (cycle_local[:, None] == jnp.arange(cycle_total, dtype=jnp.int32)[None, :]).astype(
        jnp.float32
    )
    cycle_sums = jnp.einsum("ksn,nr->ksr", statistics, cycle_hot, precision=highest)
    merged_power = jnp.sum(merged * merged, axis=1)
    merged_sums = jnp.einsum("kn,nr->kr", merged_power, cycle_hot, precision=highest)
    cycle_totals = lax.psum(jnp.concatenate([cycle_sums, merged_sums[:, None]], axis=1), "cls")
    correlation = cycle_totals[:, 0] / jnp.sqrt(
        (cycle_totals[:, 1] + noise[None, :]) * (cycle_totals[:, 2] + noise[None, :])
    )
    gain = jnp.maximum(correlation, GAIN_FLOOR)
    power_mean = jnp.sum(gain * gain * cycle_totals[:, 3], axis=1) / (2.0 * pixels)
    scale = gain / jnp.sqrt(power_mean + EPSILON)[:, None]
    scale_pixels = jnp.dot(scale, cycle_hot.T, precision=highest)
    normalized = (merged * scale_pixels[:, None, :]).astype(jnp.bfloat16)
    gathered = lax.all_gather(normalized, ("dom", "cls"), axis=0, tiled=False)
    gathered = gathered.reshape(dom_count, -1, owned_rows // 2, channels, local_pixels)
    return jnp.transpose(gathered, (0, 2, 3, 1, 4)).reshape(K, channels, pixels)


def solution(mesh):
    placed = (P("dom", None, "cls"), P("dom"), P("dom"), P("dom"), P("dom"), P(), P())
    return jax.shard_map(local, mesh=mesh, in_specs=placed, out_specs=P(), check_vma=False)
```

time: 1080 us -> 887 us (0.82)
  blocking collectives: 336 us -> 28.6 us
  waiting for transfers between devices: 655 us -> 783 us
    psum x1 -> x0, waiting for transfers between devices: 408 us -> none  [local(): summed = lax.psum(partial_sums, 'dom')]
    unnamed x2 -> x3, waiting for transfers between devices: 0.03 us -> 363 us
    psum x2 -> x1, blocking collectives: 280 us -> 28.6 us  [local(): lax.psum(jnp.concatenate([cycle_sums, merged_sums[:, None]], axis=1), 'cls')]
    all_gather x1, waiting for transfers between devices: 172 us -> 420 us  [local(): gathered = lax.all_gather(normalized, ('dom', 'cls'), axis=0, tiled=False)]
    all_to_all x1, waiting for transfers between devices: 74.9 us -> 0.01 us  [local(): lax.all_to_all(message.reshape(dom_count, owned_rows, -1), 'dom', split_a...]
    all_gather x1 -> x0, blocking collectives: 56.2 us -> none  [local(): every_class = lax.all_gather(normalized, 'cls', axis=0, tiled=True)]
    all_gather x2 -> x1, local copies, waits for them, and re-layouts: 22.5 us -> 2.8 us  [local(): gathered = lax.all_gather(normalized, ('dom', 'cls'), axis=0, tiled=False)]
    reshape x0 -> x4, local copies, waits for them, and re-layouts: none -> 13.6 us  [the longest x2 13.5 us: local(): return jnp.transpose(gathered, (0, 2, 3, 1, 4)).reshape(K, channels, pixels)]
  transfers between devices with their start and end apart: 3 -> 3, of which waited for: 3 -> 2; matrix products, arithmetic and copies ran while one was open for 0% -> 0% of each run, Pallas kernels for 0% -> 0%
where the time goes in v1:
time: 887 us; the launch traced here: 879 us
  waiting for transfers between devices  783 us (88%)
  blocking collectives  28.6 us (3%)
  local copies, waits for them, and re-layouts  24.6 us (3%)
  between operations  14.3 us (2%)
  starting transfers between devices  13.5 us (2%)
  matrix products  12.7 us (1%)
    all_gather x1, waiting for transfers between devices, local(): gathered = lax.all_gather(normalized, ('dom', 'cls'), axis=0, tiled=False)  420 us
    unnamed x3, waiting for transfers between devices  363 us
    psum x1, blocking collectives, local(): lax.psum(jnp.concatenate([cycle_sums, merged_sums[:, None]], axis=1), 'cls')  28.6 us
  transfers between devices with their start and end apart: 3, of which 2 were waited for; matrix products, arithmetic and copies ran while one was open for 0% of the time, Pallas kernels for 0%

profile of v1, /device:TPU:25, one launch (start us, length us, event | category | flops | bytes accessed | tf_op | source)
XLA Modules:
  0.0 879.4 jit_solution(14814505360475722857)
XLA Ops:
  6.5 0.7 multiply_add_fusion
  7.2 1.3 subtract_convert_fusion
  8.5 2.3 fusion.12
  10.8 6.0 fusion.2
  16.9 1.6 copy.26
  18.5 0.9 concatenate.14
  19.4 0.1 copy.27
  19.6 0.1 copy.28
  19.7 3.0 concatenate.17
  22.7 13.4 %all-to-all-start = ((bf16[32,4,4160]{2,1,0:T(4,128)(2,1)}), bf16[32,4,4160]{2,1,0:T(4,128)(2,1)S(1)}, u32[]{:S(2)}, u32[]{:S(2)}) async-start(bf16[32,4,4160]{2,1,0:T(4,128)(2,1)} %concatenate.17), calls=%async_computation | async-start | bytes 2162688 | tf_op jit(solution)/shard_map/all_to_all | solution.py:41
  36.1 0.0 all-reduce.3.cloned.1.call-start
  36.1 0.7 dynamic-slice
  37.5 0.3 dynamic-update-slice
  37.8 0.6 copy-done
  38.5 0.0 all-gather.2.cloned.1.call-start
  38.5 363.3 %all-reduce.3.cloned.1.call-done = s32[16512]{0:T(1024)} async-done(((s32[16512]{0:T(1024)}), s32[16512]{0:T(1024)}) %all-reduce.3.cloned.1.call-update) | async-done | bytes 66064
  401.9 0.8 dynamic_slice.7
  402.6 0.4 convert_reduce_fusion
  403.1 1.1 fusion.19
  404.3 0.1 reshape.70
  404.5 0.2 multiply_reduce_fusion.2
  404.7 0.1 fusion.29
  404.8 0.6 fusion.4
  405.4 0.6 fusion.6
  406.0 28.6 %psum.7 = f32[2,4,128]{2,1,0:T(4,128)S(1)} all-reduce(f32[2,4,128]{2,1,0:T(4,128)S(1)} %pad_maximum_fusion), channel_id=1, replica_groups=mesh['dom'=32,'cls'=8] {'cls'}, use_global_device_ids=true, to_apply=%region_5.0 | all-reduce | flops 1024 | bytes 8192 | tf_op jit(solution)/shard_map/psum | solution.py:66
  434.7 0.1 multiply_reduce_fusion.3
  434.8 0.7 fusion.3
  435.5 0.7 fusion.28
  436.2 420.1 %all-gather.2.cloned.1.call-done = bf16[256,2,2,2064]{3,2,1,0:T(2,128)(2,1)} async-done(((bf16[1,2,2,2064]{3,2,1,0:T(2,128)(2,1)}), bf16[256,2,2,2064]{3,2,1,0:T(2,128)(2,1)}) %all-gather.2.cloned.1.call-update) | async-done | bytes 4227088 | tf_op jit(solution)/shard_map/all_gather | solution.py:75
  856.3 2.8 copy.43
  859.1 2.4 copy.35
  861.5 11.1 %reshape.81 = bf16[64,2,16512]{2,1,0:T(2,128)(2,1)} reshape(bf16[32,2,2,8,2064]{4,3,2,1,0:T(8,128)(2,1)} %copy.35) | data formatting | bytes 8454144 | tf_op jit(solution)/shard_map/reshape | solution.py:77
  (22 shorter events, 0.3 us)
Async XLA Ops:
  16.9 19.3 %copy-start.3 = (u32[256]{0:T(256)S(1)}, u32[256]{0:T(256)}, u32[]{:S(2)}) copy-start(u32[256]{0:T(256)} %constant.32) | copy-start | bytes 3076
  16.9 20.6 %copy-start.1 = (s32[516]{0:T(1024)S(1)}, s32[516]{0:T(1024)}, u32[]{:S(2)}) copy-start(s32[516]{0:T(1024)} %param.11) | copy-start | bytes 6196
  19.4 415.2 %copy-start.2 = (f32[128]{0:T(128)S(1)}, f32[128]{0:T(128)}, u32[]{:S(2)}) copy-start(f32[128]{0:T(128)} %param.13) | copy-start | bytes 1540
  22.7 380.0 %all-to-all-start = ((bf16[32,4,4160]{2,1,0:T(4,128)(2,1)}), bf16[32,4,4160]{2,1,0:T(4,128)(2,1)S(1)}, u32[]{:S(2)}, u32[]{:S(2)}) async-start(bf16[32,4,4160]{2,1,0:T(4,128)(2,1)} %concatenate.17), calls=%async_computation | async-start | bytes 2162688 | tf_op jit(solution)/shard_map/all_to_all | solution.py:41
  36.1 365.8 %all-reduce.3.cloned.1.call-start = ((), (), s32[]{:S(2)}) async-start(), calls=%async_computation.2 | async-start | bytes 139264
  37.8 0.6 copy-start
  38.5 817.8 %all-gather.2.cloned.1.call-start = ((), (), s32[]{:S(2)}) async-start(), calls=%async_computation.1 | async-start | bytes 4473856 | tf_op jit(solution)/shard_map/all_gather | solution.py:75
Sparse Core Ops, SparseCore 0:
  39.5 362.2 all-reduce.2
  436.3 419.9 all-gather.1

commit v2 on v1

v2 whole, which is shorter than its diff:
```python
import functools

import jax
import jax.numpy as jnp
from jax import lax
from jax.experimental import pallas as pl
from jax.experimental.pallas import tpu as pltpu
from jax.sharding import PartitionSpec as P

K = 64
RIDGE = 1.0
GAIN_FLOOR = 0.02
EPSILON = 1e-06
STEP = 32
NY, NZ, NX, NC = 4, 2, 4, 2
MESH = pl.DeviceIdType.MESH


def gather_kernel(unit_ref, out_ref, own_sem, z_send, z_recv, x_send, x_recv, y_send, y_recv, c_send, c_recv):
    dom = lax.axis_index("dom")
    cls = lax.axis_index("cls")
    y = lax.div(dom, NZ * NX)
    z = lax.rem(lax.div(dom, NX), NZ)
    x = lax.rem(dom, NX)
    core = lax.rem(cls, NC)
    other = 1 - z

    def at(yy, zz, xx):
        return ((yy * NZ + zz) * NX + xx, cls)

    partner = (dom, cls + 1 - 2 * core)
    z_peer = at(y, other, x)
    x_peers = [at(y, z, lax.rem(x + j, NX)) for j in range(1, NX)]
    y_peers = [at(lax.rem(y + j, NY), z, x) for j in range(1, NY)]
    x_from = [lax.rem(x + NX - j, NX) for j in range(1, NX)]
    y_from = [lax.rem(y + NY - j, NY) for j in range(1, NY)]

    barrier = pltpu.get_barrier_semaphore()
    everyone = [partner, z_peer] + x_peers + y_peers
    for peer in everyone:
        pl.semaphore_signal(barrier, inc=1, device_id=peer, device_id_type=MESH)
    pl.semaphore_wait(barrier, len(everyone))

    def send(src, dst, send_sem, recv_sem, peer):
        copy = pltpu.make_async_remote_copy(
            src_ref=src, dst_ref=dst, send_sem=send_sem, recv_sem=recv_sem,
            device_id=peer, device_id_type=MESH,
        )
        copy.start()
        return copy

    mine = out_ref.at[y, z, x, core]
    own = pltpu.make_async_copy(unit_ref, mine, own_sem)
    own.start()
    to_z = send(unit_ref, mine, z_send, z_recv, z_peer)
    first_x = [
        send(unit_ref, mine, x_send.at[j], x_recv.at[j], x_peers[j]) for j in range(NX - 1)
    ]
    to_z.wait_recv()
    cross = out_ref.at[y, other, x, core]
    first_y = [send(cross, cross, y_send.at[j], y_recv.at[j], y_peers[j]) for j in range(NY - 1)]
    own.wait()
    for copy in first_x:
        copy.wait_recv()
    row = out_ref.at[y, z, :, core]
    second_y = [
        send(row, row, y_send.at[NY - 1 + j], y_recv.at[NY - 1 + j], y_peers[j])
        for j in range(NY - 1)
    ]
    to_core = [send(row, row, c_send.at[0], c_recv.at[0], partner)]
    for copy in first_y:
        copy.wait_recv()
    column = out_ref.at[:, other, x, core]
    second_x = [
        send(column, column, x_send.at[NX - 1 + j], x_recv.at[NX - 1 + j], x_peers[j])
        for j in range(NX - 1)
    ]
    to_core.append(send(column, column, c_send.at[1], c_recv.at[1], partner))
    for j in range(NY - 1):
        second_y[j].wait_recv()
        far = out_ref.at[y_from[j], z, :, core]
        to_core.append(send(far, far, c_send.at[2 + j], c_recv.at[2 + j], partner))
    for j in range(NX - 1):
        second_x[j].wait_recv()
        far = out_ref.at[:, other, x_from[j], core]
        slot = 1 + NY + j
        to_core.append(send(far, far, c_send.at[slot], c_recv.at[slot], partner))
    for copy in to_core:
        copy.wait_recv()
    for copy in [to_z] + first_x + first_y + second_y + second_x + to_core:
        copy.wait_send()


def gather(unit):
    channels, pixels = unit.shape
    dma = pltpu.SemaphoreType.DMA
    out = pl.pallas_call(
        gather_kernel,
        out_shape=jax.ShapeDtypeStruct((NY, NZ, NX, NC, channels, pixels), unit.dtype),
        in_specs=[pl.BlockSpec(memory_space=pl.ANY)],
        out_specs=pl.BlockSpec(memory_space=pl.ANY),
        scratch_shapes=[
            dma,
            dma,
            dma,
            dma((2 * (NX - 1),)),
            dma((2 * (NX - 1),)),
            dma((2 * (NY - 1),)),
            dma((2 * (NY - 1),)),
            dma((NX + NY,)),
            dma((NX + NY,)),
        ],
        compiler_params=pltpu.CompilerParams(collective_id=0, has_side_effects=True),
    )(unit)
    return out.reshape(NY * NZ * NX * NC, channels, pixels)


def split(value):
    parts = []
    for _ in range(3):
        part = lax.reduce_precision(value, 8, 7)
        parts.append(part.astype(jnp.bfloat16))
        value = value - part
    return jnp.concatenate(parts, axis=0)


def local(spectra, classes, halves, groups, cycles, ctf_table, noise):
    highest = lax.Precision.HIGHEST
    local_particles, channels, local_pixels = spectra.shape
    depth = ctf_table.shape[0]
    pixels = ctf_table.shape[1]
    cycle_total = noise.shape[0]
    dom_count = lax.axis_size("dom")
    cls_count = lax.axis_size("cls")
    owned_rows = 2 * K // dom_count
    width = channels * local_pixels
    pixel_begin = lax.axis_index("cls") * local_pixels
    ctf_local = lax.dynamic_slice_in_dim(ctf_table, pixel_begin, local_pixels, 1)
    group_hot = (groups[:, None] == jnp.arange(depth, dtype=jnp.int32)[None, :]).astype(
        jnp.bfloat16
    )
    labels = classes * 2 + halves
    class_hot = (labels[:, None] == jnp.arange(2 * K, dtype=jnp.int32)[None, :]).astype(
        jnp.bfloat16
    )
    ctf = jnp.dot(group_hot, ctf_local, preferred_element_type=jnp.float32)
    weighted = (ctf[:, None, :] * spectra).astype(jnp.bfloat16)
    partial_sums = jnp.einsum("pm,pcn->mcn", class_hot, weighted, preferred_element_type=jnp.float32)
    counts = jnp.einsum("pm,pg->mg", class_hot, group_hot, preferred_element_type=jnp.float32)
    high = jnp.floor(counts / STEP)
    low = counts - high * STEP
    shared = cycles.astype(jnp.float32).reshape(owned_rows, -1)
    shared = jnp.tile(shared, (dom_count, 1))
    message = jnp.concatenate(
        [partial_sums.reshape(2 * K, width), high, low, shared], axis=1
    ).astype(jnp.bfloat16)
    received = lax.all_to_all(
        message.reshape(dom_count, owned_rows, -1), "dom", split_axis=0, concat_axis=0, tiled=True
    )
    every_cycle = received[:, :, width + 2 * depth :].astype(jnp.int32).reshape(pixels)
    total = jnp.sum(received[:, :, : width + 2 * depth].astype(jnp.float32), axis=0)
    count_total = total[:, width : width + depth] * STEP + total[:, width + depth :]
    outgoing = total[:, :width].reshape(1, NC, 2 * channels, local_pixels)
    outgoing = jnp.tile(outgoing, (cls_count // NC, 1, 1, 1)).reshape(
        cls_count, 2 * channels, local_pixels
    )
    incoming = lax.all_to_all(outgoing, "cls", split_axis=0, concat_axis=0, tiled=True)
    sums = jnp.transpose(incoming, (1, 0, 2)).reshape(2, channels, pixels)
    core = lax.rem(lax.axis_index("cls"), NC)
    count_mine = lax.dynamic_slice_in_dim(count_total, core * 2, 2, 0)
    square_table = (ctf_table.astype(jnp.float32) ** 2).astype(jnp.bfloat16)
    parts = jnp.dot(split(count_mine), square_table, preferred_element_type=jnp.float32)
    wsum = parts.reshape(3, 2, pixels).sum(axis=0)
    halfavg = sums / (wsum[:, None, :] + RIDGE)
    merged = (sums[0] + sums[1]) / (wsum[0] + wsum[1] + RIDGE)[None, :]
    statistics = jnp.stack(
        [
            jnp.sum(halfavg[0] * halfavg[1], axis=0),
            jnp.sum(halfavg[0] * halfavg[0], axis=0),
            jnp.sum(halfavg[1] * halfavg[1], axis=0),
            jnp.sum(merged * merged, axis=0),
        ],
        axis=0,
    )
    rings = jnp.arange(cycle_total, dtype=jnp.int32)
    cycle_hot = (rings[:, None] == every_cycle[None, :]).astype(jnp.bfloat16)
    totals = jnp.einsum("sn,rn->sr", split(statistics), cycle_hot, preferred_element_type=jnp.float32)
    totals = totals.reshape(3, 4, cycle_total).sum(axis=0)
    correlation = totals[0] / jnp.sqrt((totals[1] + noise) * (totals[2] + noise))
    gain = jnp.maximum(correlation, GAIN_FLOOR)
    power_mean = jnp.sum(gain * gain * totals[3]) / (2.0 * pixels)
    scale = (gain / jnp.sqrt(power_mean + EPSILON))[None, :]
    scale_pixels = jnp.sum(
        jnp.dot(split(scale), cycle_hot, preferred_element_type=jnp.float32), axis=0
    )
    return gather((merged * scale_pixels[None, :]).astype(jnp.bfloat16))


def solution(mesh):
    placed = (P("dom", None, "cls"), P("dom"), P("dom"), P("dom"), P("dom"), P(), P())
    return jax.shard_map(local, mesh=mesh, in_specs=placed, out_specs=P(), check_vma=False)
```

time: 887 us -> 125 us (0.14)
  waiting for transfers between devices: 783 us -> 28.6 us
  Pallas kernels: 0 us -> 33.9 us
  blocking collectives: 28.6 us -> 0 us
  starting transfers between devices: 13.5 us -> 28 us
  between operations: 14.3 us -> 0.95 us
  local copies, waits for them, and re-layouts: 24.6 us -> 15.5 us
    all_gather x1 -> x0, waiting for transfers between devices: 420 us -> none  [local(): gathered = lax.all_gather(normalized, ('dom', 'cls'), axis=0, tiled=False)]
    unnamed x3 -> x0, waiting for transfers between devices: 363 us -> none
    pallas_call x0 -> x1, Pallas kernels: none -> 33.9 us  [gather(): pl.pallas_call(gather_kernel, out_shape=jax.ShapeDtypeStruct((NY, NZ, NX,...]
    psum x1 -> x0, blocking collectives: 28.6 us -> none  [local(): lax.psum(jnp.concatenate([cycle_sums, merged_sums[:, None]], axis=1), 'cls')]
    all_to_all x1, waiting for transfers between devices: 0.01 us -> 20.7 us  [local(): lax.all_to_all(message.reshape(dom_count, owned_rows, -1), 'dom', split_a...]
    all_to_all x0 -> x1, starting transfers between devices: none -> 14.5 us  [local(): lax.all_to_all(outgoing, 'cls', split_axis=0, concat_axis=0, tiled=True)]
    reshape x4 -> x3, local copies, waits for them, and re-layouts: 13.6 us -> 0.61 us  [the longest x1 0.37 us: local(): sums = jnp.transpose(incoming, (1, 0, 2)).reshape(2, channels, pixels)]
  transfers between devices with their start and end apart: 3 -> 2, of which waited for: 2 -> 2; matrix products, arithmetic and copies ran while one was open for 0% -> 1% of each run, Pallas kernels for 0% -> 0%
where the time goes in v2:
time: 125 us; the launch traced here: 124 us
  Pallas kernels  33.9 us (27%)
  waiting for transfers between devices  28.6 us (23%)
  starting transfers between devices  28 us (22%)
  local copies, waits for them, and re-layouts  15.5 us (12%)
  matrix products  12.8 us (10%)
  other arithmetic  4.56 us (4%)
    pallas_call x1, Pallas kernels, gather(): pl.pallas_call(gather_kernel, out_shape=jax.ShapeDtypeStruct((NY, NZ, NX,...  33.9 us
    all_to_all x1, waiting for transfers between devices, local(): lax.all_to_all(message.reshape(dom_count, owned_rows, -1), 'dom', split_a...  20.7 us
    all_to_all x1, starting transfers between devices, local(): lax.all_to_all(outgoing, 'cls', split_axis=0, concat_axis=0, tiled=True)  14.5 us
    all_to_all x1, starting transfers between devices, local(): lax.all_to_all(message.reshape(dom_count, owned_rows, -1), 'dom', split_a...  13.5 us
    all_to_all x1, waiting for transfers between devices, local(): lax.all_to_all(outgoing, 'cls', split_axis=0, concat_axis=0, tiled=True)  7.93 us
    unnamed x7, local copies, waits for them, and re-layouts  7.14 us
    dot_general x1, matrix products, local(): jnp.einsum('pm,pcn->mcn', class_hot, weighted, preferred_element_type=jnp...  6.03 us
    concatenate x2, local copies, waits for them, and re-layouts, local(): jnp.concatenate([partial_sums.reshape(2 * K, width), high, low, shared],...  4 us
  transfers between devices with their start and end apart: 2, of which 2 were waited for; matrix products, arithmetic and copies ran while one was open for 1% of the time, Pallas kernels for 0%

profile of v2, /device:TPU:25, one launch (start us, length us, event | category | flops | bytes accessed | tf_op | source)
XLA Modules:
  0.0 124.4 jit_solution(3658609035846006091)
XLA Ops:
  0.0 0.7 multiply_add_fusion
  0.7 1.3 %subtract_convert_fusion = (bf16[128,16]{0,1:T(8,128)(2,1)S(1)}, bf16[128,16]{0,1:T(8,128)(2,1)S(1)}) fusion(s32[1024]{0:T(1024)} %param.10, s32[1024]{0:T(1024)S(1)} %multiply_add_fusion), kind=kOutput, calls=%fused_computation.48 | convolution fusion | flops 4354048 | bytes 16384 | tf_op jit(solution)/shard_map/pm,pg->mg/dot_general | solution.py:149
  2.0 2.3 %fusion.15 = f32[1024,2064]{0,1:T(8,128)S(1)} fusion(s32[1024]{0:T(1024)} %param.10, bf16[16,16512]{1,0:T(8,128)(2,1)} %param.12, s32[]{:T(128)S(6)} %select_n.6), kind=kOutput, calls=%fused_computation.20 | convolution fusion | flops 67649536 | bytes 8527876 | tf_op jit(solution)/shard_map/dot_general | solution.py:146
  4.3 6.0 %fusion.6 = bf16[128,2,2064]{0,2,1:T(8,128)(2,1)S(1)} fusion(bf16[1024,2,2064]{0,2,1:T(8,128)(2,1)} %param.7, f32[1024,2064]{0,1:T(8,128)S(1)} %fusion.15, s32[1024]{0:T(1024)S(1)} %multiply_add_fusion), kind=kOutput, calls=%fused_computation.8 | convolution fusion | flops 1095471104 | bytes 17969152 | tf_op jit(solution)/shard_map/pm,pcn->mcn/dot_general | solution.py:148
  10.4 1.6 %copy.16 = bf16[128,2,2064]{2,1,0:T(2,128)(2,1)S(1)} copy(bf16[128,2,2064]{0,2,1:T(8,128)(2,1)S(1)} %fusion.6) | data formatting | bytes 2113536 | tf_op jit(solution)/shard_map/convert.7
  12.0 0.9 concatenate.20
  12.9 0.1 copy.17
  13.3 3.1 %concatenate.23 = bf16[32,4,4289]{2,1,0:T(4,128)(2,1)} concatenate(bf16[32,4,4128]{2,1,0:T(4,128)(2,1)S(1)} %concatenate.20, bf16[32,4,16]{2,1,0:T(4,128)(2,1)S(1)} %bitcast.46, bf16[32,4,16]{2,1,0:T(4,128)(2,1)S(1)} %bitcast.47, bf16[32,4,129]{2,1,0:T(4,128)(2,1)S(1)} %tile.18), dimensions={2} | concatenate | bytes 2195968 | tf_op jit(solution)/shard_map/concatenate | solution.py:154
  16.4 13.5 %all-to-all-start = ((bf16[32,4,4289]{2,1,0:T(4,128)(2,1)}), bf16[32,4,4289]{2,1,0:T(4,128)(2,1)S(1)}, u32[]{:S(2)}, u32[]{:S(2)}) async-start(bf16[32,4,4289]{2,1,0:T(4,128)(2,1)} %concatenate.23), calls=%async_computation | async-start | bytes 2228224 | tf_op jit(solution)/shard_map/all_to_all | solution.py:157
  29.9 20.7 %all-to-all-done = bf16[32,4,4289]{2,1,0:T(4,128)(2,1)S(1)} async-done(((bf16[32,4,4289]{2,1,0:T(4,128)(2,1)}), bf16[32,4,4289]{2,1,0:T(4,128)(2,1)S(1)}, u32[]{:S(2)}, u32[]{:S(2)}) %all-to-all-start) | async-done | bytes 1098016 | tf_op jit(solution)/shard_map/all_to_all | solution.py:157
  50.6 0.4 convert_reduce_fusion
  51.1 0.2 fusion.8
  51.4 0.2 reshape.63
  51.7 0.7 tile.20
  52.5 14.5 %all-to-all-start.1 = ((f32[8,4,2064]{2,1,0:T(4,128)}), f32[8,4,2064]{2,1,0:T(4,128)S(1)}, u32[]{:S(2)}, u32[]{:S(2)}) async-start(f32[8,4,2064]{2,1,0:T(4,128)} %bitcast.3), calls=%async_computation.1 | async-start | bytes 557056 | tf_op jit(solution)/shard_map/all_to_all | solution.py:167
  66.9 0.3 reduce_sum.82
  67.2 0.2 fusion.27
  67.7 0.3 reshape.68
  68.0 7.9 %all-to-all-done.1 = f32[8,4,2064]{2,1,0:T(4,128)S(1)} async-done(((f32[8,4,2064]{2,1,0:T(4,128)}), f32[8,4,2064]{2,1,0:T(4,128)S(1)}, u32[]{:S(2)}, u32[]{:S(2)}) %all-to-all-start.1) | async-done | bytes 264224 | tf_op jit(solution)/shard_map/all_to_all | solution.py:167
  76.0 0.4 reshape.64
  76.3 0.1 broadcast_divide_fusion
  76.5 0.5 multiply_reduce_fusion.2
  77.2 0.3 fusion.24
  77.4 0.1 stack.18
  77.6 0.4 reduce-precision_convert_fusion.1
  78.0 1.5 %fusion.2 = f32[12,128]{1,0:T(8,128)S(1)} fusion(s32[16512]{0:T(1024)S(1)} %reshape.68, bf16[4,16512]{1,0:T(4,128)(2,1)S(1)} %get-tuple-element.16, bf16[4,16512]{1,0:T(4,128)(2,1)S(1)} %get-tuple-element.15, bf16[4,16512]{1,0:T(4,128)(2,1)S(1)} %get-tuple-element.14), kind=kOutput, calls=%fused_computation.4 | convolution fusion | flops 54027264 | bytes 468480 | tf_op jit(solution)/shard_map/sn,rn->sr/dot_general | solution.py:187
  79.6 0.6 fusion.46
  80.9 0.2 add.53
  81.1 1.5 %fusion.7 = f32[16512]{0:T(1024)S(1)} fusion(s32[16512]{0:T(1024)S(1)} %reshape.68, bf16[1,128]{1,0:T(2,128)(2,1)S(1)} %get-tuple-element.23, bf16[1,128]{1,0:T(2,128)(2,1)S(1)} %get-tuple-element.22, bf16[1,128]{1,0:T(2,128)(2,1)S(1)} %get-tuple-element.8), kind=kOutput, calls=%fused_computation.10 | convolution fusion | flops 14830080 | bytes 132864 | tf_op jit(solution)/shard_map/dot_general | solution.py:194
  82.6 0.7 multiply_convert_fusion.6.unit_ref
  83.3 33.9 %shard_map.73 = bf16[4,2,4,2,2,16512]{5,4,3,2,1,0:T(2,128)(2,1)} custom-call(bf16[2,16512]{1,0:T(2,128)(2,1)} %multiply_convert_fusion.6.unit_ref), custom_call_target="tpu_custom_call" | custom-call | tf_op jit(solution)/shard_map/pallas_call | solution.py:97
  117.2 7.1 %copy.22 = bf16[64,2,16512]{2,1,0:T(2,128)(2,1)} copy(bf16[64,2,16512]{2,1,0:T(2,128)(2,1)} %bitcast.42) | data formatting | bytes 8454144
  (25 shorter events, 1.0 us)
Async XLA Ops:
  10.3 2.8 %copy-start.1 = (s32[516]{0:T(1024)S(1)}, s32[516]{0:T(1024)}, u32[]{:S(2)}) copy-start(s32[516]{0:T(1024)} %param.11) | copy-start | bytes 6196
  16.4 34.8 %copy-start = (bf16[16,16512]{1,0:T(8,128)(2,1)S(1)}, bf16[16,16512]{1,0:T(8,128)(2,1)}, u32[]{:S(2)}) copy-start(bf16[16,16512]{1,0:T(8,128)(2,1)} %param.12) | copy-start | bytes 1585156
  16.4 34.2 %all-to-all-start = ((bf16[32,4,4289]{2,1,0:T(4,128)(2,1)}), bf16[32,4,4289]{2,1,0:T(4,128)(2,1)S(1)}, u32[]{:S(2)}, u32[]{:S(2)}) async-start(bf16[32,4,4289]{2,1,0:T(4,128)(2,1)} %concatenate.23), calls=%async_computation | async-start | bytes 2228224 | tf_op jit(solution)/shard_map/all_to_all | solution.py:157
  52.5 23.5 %all-to-all-start.1 = ((f32[8,4,2064]{2,1,0:T(4,128)}), f32[8,4,2064]{2,1,0:T(4,128)S(1)}, u32[]{:S(2)}, u32[]{:S(2)}) async-start(f32[8,4,2064]{2,1,0:T(4,128)} %bitcast.3), calls=%async_computation.1 | async-start | bytes 557056 | tf_op jit(solution)/shard_map/all_to_all | solution.py:167
  77.6 2.0 %copy-start.2 = (f32[128]{0:T(128)S(1)}, f32[128]{0:T(128)}, u32[]{:S(2)}) copy-start(f32[128]{0:T(128)} %param.13) | copy-start | bytes 1540

commit v3 on v2

--- a/solution.py
+++ b/solution.py
@@ -11,7 +11,8 @@
 RIDGE = 1.0
 GAIN_FLOOR = 0.02
 EPSILON = 1e-06
-STEP = 32
+STEP = 16
+LANES = 128
 NY, NZ, NX, NC = 4, 2, 4, 2
 MESH = pl.DeviceIdType.MESH
 
@@ -110,9 +111,130 @@
             dma((NX + NY,)),
             dma((NX + NY,)),
         ],
-        compiler_params=pltpu.CompilerParams(collective_id=0, has_side_effects=True),
+        compiler_params=pltpu.CompilerParams(
+            collective_id=0, has_side_effects=True, vmem_limit_bytes=8 << 20
+        ),
     )(unit)
     return out.reshape(NY * NZ * NX * NC, channels, pixels)
+
+
+def reduce_kernel(
+    message_ref, cycles_ref, out_ref, cycles_out_ref,
+    got, staged, far,
+    own_sem, plane_send, plane_recv, column_send, column_recv, cycle_send, cycle_recv,
+):
+    dom = lax.axis_index("dom")
+    cls = lax.axis_index("cls")
+    y = lax.div(dom, NZ * NX)
+    z = lax.rem(lax.div(dom, NX), NZ)
+    x = lax.rem(dom, NX)
+    core = lax.rem(cls, NC)
+    groups = far.shape[1]
+    rows = far.shape[2]
+    doms = NY * NZ * NX
+
+    plane = []
+    for dy in range(NY):
+        for dx in range(NX):
+            plane.append((lax.rem(y + dy, NY), lax.rem(x + dx, NX)))
+    column = []
+    for dz in range(NZ):
+        for dc in range(groups):
+            column.append((lax.rem(z + dz, NZ), lax.rem(cls + dc, groups)))
+    others = [lax.rem(dom + step, doms) for step in range(1, doms)]
+
+    barrier = pltpu.get_barrier_semaphore()
+    greeted = [(there, cls) for there in others]
+    for step, (zz, cc) in enumerate(column):
+        if step % groups:
+            greeted.append(((y * NZ + zz) * NX + x, cc))
+    for peer in greeted:
+        pl.semaphore_signal(barrier, inc=1, device_id=peer, device_id_type=MESH)
+    pl.semaphore_wait(barrier, len(greeted))
+
+    own = pltpu.make_async_copy(message_ref.at[y, :, x], got.at[0], own_sem.at[0])
+    own.start()
+    own_cycles = pltpu.make_async_copy(cycles_ref, cycles_out_ref.at[dom], own_sem.at[1])
+    own_cycles.start()
+    sends = []
+    for step in range(1, NY * NX):
+        yy, xx = plane[step]
+        copy = pltpu.make_async_remote_copy(
+            src_ref=message_ref.at[yy, :, xx], dst_ref=got.at[step],
+            send_sem=plane_send.at[step], recv_sem=plane_recv.at[step],
+            device_id=((yy * NZ + z) * NX + xx, cls), device_id_type=MESH,
+        )
+        copy.start()
+        sends.append(copy)
+    for there in others:
+        pltpu.make_async_remote_copy(
+            src_ref=cycles_ref, dst_ref=cycles_out_ref.at[dom],
+            send_sem=cycle_send, recv_sem=cycle_recv,
+            device_id=(there, cls), device_id_type=MESH,
+        ).start()
+    own.wait()
+    for copy in sends:
+        copy.wait_recv()
+    for zz in range(NZ):
+        total = got[0, zz].astype(jnp.float32)
+        for step in range(1, NY * NX):
+            total = total + got[step, zz].astype(jnp.float32)
+        total = total.astype(jnp.bfloat16)
+        for cc in range(NC):
+            staged[zz, cc] = total[cc * rows : (cc + 1) * rows]
+    kept = pltpu.make_async_copy(staged.at[z, core], far.at[z, cls], own_sem.at[2])
+    kept.start()
+    relays = []
+    for step in range(1, NZ * groups):
+        zz, cc = column[step]
+        copy = pltpu.make_async_remote_copy(
+            src_ref=staged.at[zz, lax.rem(cc, NC)], dst_ref=far.at[z, cls],
+            send_sem=column_send.at[step], recv_sem=column_recv.at[step],
+            device_id=((y * NZ + zz) * NX + x, cc), device_id_type=MESH,
+        )
+        copy.start()
+        relays.append(copy)
+    kept.wait()
+    for copy in relays:
+        copy.wait_recv()
+    for cc in range(groups):
+        out_ref[cc] = far[0, cc].astype(jnp.float32) + far[1, cc].astype(jnp.float32)
+    own_cycles.wait()
+    span = cycles_out_ref.at[pl.ds(0, doms - 1)]
+    pltpu.make_async_copy(span, span, cycle_recv).wait()
+    pltpu.make_async_copy(span, span, cycle_send).wait()
+    for copy in sends + relays:
+        copy.wait_send()
+
+
+def reduce(message, cycles, groups):
+    doms, rows, width = message.shape
+    dma = pltpu.SemaphoreType.DMA
+    half = rows // NC
+    return pl.pallas_call(
+        reduce_kernel,
+        out_shape=(
+            jax.ShapeDtypeStruct((groups, half, width), jnp.float32),
+            jax.ShapeDtypeStruct((doms,) + cycles.shape, cycles.dtype),
+        ),
+        in_specs=[pl.BlockSpec(memory_space=pltpu.VMEM)] * 2,
+        out_specs=(pl.BlockSpec(memory_space=pltpu.VMEM),) * 2,
+        scratch_shapes=[
+            pltpu.VMEM((NY * NX, NZ, rows, width), jnp.bfloat16),
+            pltpu.VMEM((NZ, NC, half, width), jnp.bfloat16),
+            pltpu.VMEM((NZ, groups, half, width), jnp.bfloat16),
+            dma((3,)),
+            dma((NY * NX,)),
+            dma((NY * NX,)),
+            dma((NZ * groups,)),
+            dma((NZ * groups,)),
+            dma,
+            dma,
+        ],
+        compiler_params=pltpu.CompilerParams(
+            collective_id=1, has_side_effects=True, vmem_limit_bytes=16 << 20
+        ),
+    )(message.reshape(NY, NZ, NX, rows, width), cycles)
 
 
 def split(value):
@@ -125,7 +247,6 @@
 
 
 def local(spectra, classes, halves, groups, cycles, ctf_table, noise):
-    highest = lax.Precision.HIGHEST
     local_particles, channels, local_pixels = spectra.shape
     depth = ctf_table.shape[0]
     pixels = ctf_table.shape[1]
@@ -133,7 +254,6 @@
     dom_count = lax.axis_size("dom")
     cls_count = lax.axis_size("cls")
     owned_rows = 2 * K // dom_count
-    width = channels * local_pixels
     pixel_begin = lax.axis_index("cls") * local_pixels
     ctf_local = lax.dynamic_slice_in_dim(ctf_table, pixel_begin, local_pixels, 1)
     group_hot = (groups[:, None] == jnp.arange(depth, dtype=jnp.int32)[None, :]).astype(
@@ -147,27 +267,26 @@
     weighted = (ctf[:, None, :] * spectra).astype(jnp.bfloat16)
     partial_sums = jnp.einsum("pm,pcn->mcn", class_hot, weighted, preferred_element_type=jnp.float32)
     counts = jnp.einsum("pm,pg->mg", class_hot, group_hot, preferred_element_type=jnp.float32)
-    high = jnp.floor(counts / STEP)
-    low = counts - high * STEP
-    shared = cycles.astype(jnp.float32).reshape(owned_rows, -1)
-    shared = jnp.tile(shared, (dom_count, 1))
+    counts = counts.astype(jnp.int32)
+    digits = jnp.concatenate(
+        [counts % STEP, (counts // STEP) % STEP, counts // (STEP * STEP)], axis=1
+    )
+    spare = -(local_pixels + 3 * depth) % LANES + 3 * depth
+    digits = jnp.pad(digits[:, None, :], ((0, 0), (0, channels - 1), (0, spare - 3 * depth)))
     message = jnp.concatenate(
-        [partial_sums.reshape(2 * K, width), high, low, shared], axis=1
-    ).astype(jnp.bfloat16)
-    received = lax.all_to_all(
-        message.reshape(dom_count, owned_rows, -1), "dom", split_axis=0, concat_axis=0, tiled=True
-    )
-    every_cycle = received[:, :, width + 2 * depth :].astype(jnp.int32).reshape(pixels)
-    total = jnp.sum(received[:, :, : width + 2 * depth].astype(jnp.float32), axis=0)
-    count_total = total[:, width : width + depth] * STEP + total[:, width + depth :]
-    outgoing = total[:, :width].reshape(1, NC, 2 * channels, local_pixels)
-    outgoing = jnp.tile(outgoing, (cls_count // NC, 1, 1, 1)).reshape(
-        cls_count, 2 * channels, local_pixels
-    )
-    incoming = lax.all_to_all(outgoing, "cls", split_axis=0, concat_axis=0, tiled=True)
-    sums = jnp.transpose(incoming, (1, 0, 2)).reshape(2, channels, pixels)
-    core = lax.rem(lax.axis_index("cls"), NC)
-    count_mine = lax.dynamic_slice_in_dim(count_total, core * 2, 2, 0)
+        [partial_sums.astype(jnp.bfloat16), digits.astype(jnp.bfloat16)], axis=2
+    )
+    cycle_rows = -(-cycles.shape[0] // (8 * LANES)) * 8
+    cycle_block = jnp.pad(cycles, (0, cycle_rows * LANES - cycles.shape[0]))
+    incoming, every_cycle = reduce(
+        message.reshape(dom_count, owned_rows * channels, local_pixels + spare),
+        cycle_block.reshape(cycle_rows, LANES),
+        cls_count,
+    )
+    every_cycle = every_cycle.reshape(dom_count, -1)[:, : cycles.shape[0]].reshape(pixels)
+    sums = jnp.transpose(incoming[:, :, :local_pixels], (1, 0, 2)).reshape(2, channels, pixels)
+    found = incoming[0, ::channels, local_pixels : local_pixels + 3 * depth].reshape(2, 3, depth)
+    count_mine = found[:, 0] + STEP * found[:, 1] + (STEP * STEP) * found[:, 2]
     square_table = (ctf_table.astype(jnp.float32) ** 2).astype(jnp.bfloat16)
     parts = jnp.dot(split(count_mine), square_table, preferred_element_type=jnp.float32)
     wsum = parts.reshape(3, 2, pixels).sum(axis=0)

time: 125 us -> 95.1 us (0.76)
  Pallas kernels: 33.9 us -> 71.7 us
  waiting for transfers between devices: 28.6 us -> 0 us
  starting transfers between devices: 28 us -> 0 us
  local copies, waits for them, and re-layouts: 15.5 us -> 5.95 us
    pallas_call x0 -> x1, Pallas kernels: none -> 34.8 us  [reduce(): pl.pallas_call(reduce_kernel, out_shape=(jax.ShapeDtypeStruct((groups, ha...]
    all_to_all x2 -> x0, waiting for transfers between devices: 28.6 us -> none  [the longest x1 20.7 us: local(): lax.all_to_all(message.reshape(dom_count, owned_rows, -1), 'dom', split_a...]
    all_to_all x2 -> x0, starting transfers between devices: 28 us -> none  [the longest x1 14.5 us: local(): lax.all_to_all(outgoing, 'cls', split_axis=0, concat_axis=0, tiled=True)]
    unnamed x7 -> x8, local copies, waits for them, and re-layouts: 7.14 us -> 2.07 us
    pallas_call x1, Pallas kernels: 33.9 us -> 36.9 us  [gather(): pl.pallas_call(gather_kernel, out_shape=jax.ShapeDtypeStruct((NY, NZ, NX,...]
    another operation x7 -> x2, local copies, waits for them, and re-layouts: 2.81 us -> 0.55 us  [the longest x1 0.47 us: reduce(): message.reshape(NY, NZ, NX, rows, width)]
    concatenate x2 -> x1, local copies, waits for them, and re-layouts: 4 us -> 1.85 us  [local(): jnp.concatenate([partial_sums.astype(jnp.bfloat16), digits.astype(jnp.bfl...]
  transfers between devices with their start and end apart: 2 -> 0, of which waited for: 2 -> 0; matrix products, arithmetic and copies ran while one was open for 1% -> 0% of each run, Pallas kernels for 0% -> 0%
where the time goes in v3:
time: 95.1 us; the launch traced here: 94.9 us
  Pallas kernels  71.7 us (75%)
  matrix products  12.9 us (14%)
  local copies, waits for them, and re-layouts  5.95 us (6%)
  other arithmetic  3.38 us (4%)
  between operations  0.99 us (1%)
    pallas_call x1, Pallas kernels, gather(): pl.pallas_call(gather_kernel, out_shape=jax.ShapeDtypeStruct((NY, NZ, NX,...  36.9 us
    pallas_call x1, Pallas kernels, reduce(): pl.pallas_call(reduce_kernel, out_shape=(jax.ShapeDtypeStruct((groups, ha...  34.8 us
    dot_general x1, matrix products, local(): jnp.einsum('pm,pcn->mcn', class_hot, weighted, preferred_element_type=jnp...  6.04 us
    dot_general x1, matrix products, local(): ctf = jnp.dot(group_hot, ctf_local, preferred_element_type=jnp.float32)  2.33 us
    unnamed x8, local copies, waits for them, and re-layouts  2.07 us

profile of v3, /device:TPU:25, one launch (start us, length us, event | category | flops | bytes accessed | tf_op | source)
XLA Modules:
  0.0 94.9 jit_solution(6587109081589774228)
XLA Ops:
  0.0 0.7 multiply_add_fusion
  0.7 1.3 %fusion.29 = (bf16[128,16]{0,1:T(8,128)(2,1)S(1)}, bf16[128,16]{0,1:T(8,128)(2,1)S(1)}, bf16[128,16]{0,1:T(8,128)(2,1)S(1)}) fusion(s32[1024]{0:T(1024)} %param.10, s32[1024]{0:T(1024)S(1)} %multiply_add_fusion), kind=kOutput, calls=%fused_computation.63 | convolution fusion | flops 4431872 | bytes 20480 | tf_op jit(solution)/shard_map/pm,pg->mg/dot_general | solution.py:269
  2.0 2.3 %fusion.16 = f32[1024,2064]{0,1:T(8,128)S(1)} fusion(s32[1024]{0:T(1024)} %param.10, bf16[16,16512]{1,0:T(8,128)(2,1)} %param.12, s32[]{:T(128)S(6)} %select_n.22), kind=kOutput, calls=%fused_computation.22 | convolution fusion | flops 67649536 | bytes 8527876 | tf_op jit(solution)/shard_map/dot_general | solution.py:266
  4.3 6.0 %fusion.6 = bf16[128,2,2064]{0,2,1:T(8,128)(2,1)S(1)} fusion(bf16[1024,2,2064]{0,2,1:T(8,128)(2,1)} %param.7, f32[1024,2064]{0,1:T(8,128)S(1)} %fusion.16, s32[1024]{0:T(1024)S(1)} %multiply_add_fusion), kind=kOutput, calls=%fused_computation.8 | convolution fusion | flops 1095471104 | bytes 17969152 | tf_op jit(solution)/shard_map/pm,pcn->mcn/dot_general | solution.py:268
  10.4 0.1 fusion.9
  10.5 0.0 copy-start.1
  10.5 1.8 %copy.10 = bf16[128,2,2176]{2,1,0:T(2,128)(2,1)S(1)} copy(bf16[128,2,2176]{0,2,1:T(8,128)(2,1)S(1)} %fusion.9) | data formatting | bytes 2228224 | tf_op jit(solution)/shard_map/concatenate | solution.py:276
  12.4 0.5 reshape_reshape.3.message_ref
  12.8 34.8 %shard_map.73 = (f32[8,4,2176]{2,1,0:T(4,128)S(1)}, s32[32,8,128]{2,1,0:T(8,128)S(1)}) custom-call(bf16[4,2,4,8,2176]{4,3,2,1,0:T(8,128)(2,1)S(1)} %reshape_reshape.3.message_ref, s32[8,128]{1,0:T(8,128)S(1)} %pad_bitcast_fusion.cycles_ref), custom_call_target="tpu_custom_call" | custom-call | tf_op jit(solution)/shard_map/pallas_call | solution.py:214
  47.6 0.1 slice.57
  47.7 0.1 reshape_squeeze.3
  47.8 0.2 fusion.10
  48.1 0.2 reshape.57
  48.3 0.3 reduce_sum.72
  48.6 0.1 broadcast_add_fusion
  48.7 0.4 reshape.58
  49.1 0.1 broadcast_divide_fusion
  49.2 0.5 multiply_reduce_fusion.2
  49.9 0.2 fusion.28
  50.1 0.1 div.72
  50.2 0.3 fusion.25
  50.5 0.1 stack.18
  50.6 0.4 reduce-precision_convert_fusion.1
  51.0 0.1 eq.51
  51.2 1.5 %fusion.2 = f32[12,128]{1,0:T(8,128)S(1)} fusion(s32[16512]{0:T(1024)S(1)} %eq.51, bf16[4,16512]{1,0:T(4,128)(2,1)S(1)} %get-tuple-element.20, bf16[4,16512]{1,0:T(4,128)(2,1)S(1)} %get-tuple-element.19, bf16[4,16512]{1,0:T(4,128)(2,1)S(1)} %get-tuple-element.18), kind=kOutput, calls=%fused_computation.4 | convolution fusion | flops 54027264 | bytes 468480 | tf_op jit(solution)/shard_map/sn,rn->sr/dot_general | solution.py:306
  52.7 0.1 reduce_sum.77
  52.8 0.6 fusion.55
  54.1 1.5 %fusion.8 = f32[16512]{0:T(1024)S(1)} fusion(s32[16512]{0:T(1024)S(1)} %eq.51, bf16[1,128]{1,0:T(2,128)(2,1)S(1)} %get-tuple-element.28, bf16[1,128]{1,0:T(2,128)(2,1)S(1)} %get-tuple-element.27, bf16[1,128]{1,0:T(2,128)(2,1)S(1)} %get-tuple-element.12), kind=kOutput, calls=%fused_computation.11 | convolution fusion | flops 14830080 | bytes 132864 | tf_op jit(solution)/shard_map/dot_general | solution.py:313
  55.6 0.2 add.75
  55.8 0.1 multiply_convert_fusion.6.unit_ref
  55.9 36.9 %shard_map.74 = bf16[4,2,4,2,2,16512]{5,4,3,2,1,0:T(2,128)(2,1)S(1)} custom-call(bf16[2,16512]{1,0:T(2,128)(2,1)S(1)} %multiply_convert_fusion.6.unit_ref), custom_call_target="tpu_custom_call" | custom-call | tf_op jit(solution)/shard_map/pallas_call | solution.py:98
  92.8 2.0 %copy.17 = bf16[64,2,16512]{2,1,0:T(2,128)(2,1)} copy(bf16[64,2,16512]{2,1,0:T(2,128)(2,1)S(1)} %bitcast.48) | data formatting | bytes 8454144
  (20 shorter events, 0.3 us)
Async XLA Ops:
  10.5 2.4 %copy-start.1 = (s32[516]{0:T(1024)S(1)}, s32[516]{0:T(1024)}, u32[]{:S(2)}) copy-start(s32[516]{0:T(1024)} %param.11) | copy-start | bytes 6196
  12.3 35.5 %copy-start = (bf16[16,16512]{1,0:T(8,128)(2,1)S(1)}, bf16[16,16512]{1,0:T(8,128)(2,1)}, u32[]{:S(2)}) copy-start(bf16[16,16512]{1,0:T(8,128)(2,1)} %param.12) | copy-start | bytes 1585156
  51.0 1.8 %copy-start.2 = (f32[128]{0:T(128)S(1)}, f32[128]{0:T(128)}, u32[]{:S(2)}) copy-start(f32[128]{0:T(128)} %param.13) | copy-start | bytes 1540

commit v4 on v3

--- a/solution.py
+++ b/solution.py
@@ -31,10 +31,12 @@
 
     partner = (dom, cls + 1 - 2 * core)
     z_peer = at(y, other, x)
-    x_peers = [at(y, z, lax.rem(x + j, NX)) for j in range(1, NX)]
-    y_peers = [at(lax.rem(y + j, NY), z, x) for j in range(1, NY)]
-    x_from = [lax.rem(x + NX - j, NX) for j in range(1, NX)]
-    y_from = [lax.rem(y + NY - j, NY) for j in range(1, NY)]
+    turn = 1 - 2 * core
+    x_next, x_last = lax.rem(x + turn + NX, NX), lax.rem(x - turn + NX, NX)
+    y_next, y_last = lax.rem(y + turn + NY, NY), lax.rem(y - turn + NY, NY)
+    x_far, y_far = lax.rem(x + 2, NX), lax.rem(y + 2, NY)
+    x_peers = [at(y, z, x_next), at(y, z, x_last)]
+    y_peers = [at(y_next, z, x), at(y_last, z, x)]
 
     barrier = pltpu.get_barrier_semaphore()
     everyone = [partner, z_peer] + x_peers + y_peers
@@ -50,45 +52,74 @@
         copy.start()
         return copy
 
+    everything = []
+
+    def to_x(src, dst, slot, back=False):
+        copy = send(src, dst, x_send.at[slot], x_recv.at[slot], x_peers[1 if back else 0])
+        everything.append(copy)
+        return copy
+
+    def to_y(src, dst, slot, back=False):
+        copy = send(src, dst, y_send.at[slot], y_recv.at[slot], y_peers[1 if back else 0])
+        everything.append(copy)
+        return copy
+
+    to_core = []
+
+    def across(ref):
+        slot = len(to_core)
+        to_core.append(send(ref, ref, c_send.at[slot], c_recv.at[slot], partner))
+
+    def row(yy):
+        return out_ref.at[yy, z, :, core]
+
+    def column(xx):
+        return out_ref.at[:, other, xx, core]
+
     mine = out_ref.at[y, z, x, core]
     own = pltpu.make_async_copy(unit_ref, mine, own_sem)
     own.start()
     to_z = send(unit_ref, mine, z_send, z_recv, z_peer)
-    first_x = [
-        send(unit_ref, mine, x_send.at[j], x_recv.at[j], x_peers[j]) for j in range(NX - 1)
-    ]
+    ahead = to_x(unit_ref, mine, 0)
+    behind = to_x(unit_ref, mine, 1, True)
+    ahead.wait_recv()
+    passed = out_ref.at[y, z, x_last, core]
+    relay_x = to_x(passed, passed, 2)
     to_z.wait_recv()
     cross = out_ref.at[y, other, x, core]
-    first_y = [send(cross, cross, y_send.at[j], y_recv.at[j], y_peers[j]) for j in range(NY - 1)]
+    up = to_y(cross, cross, 0)
+    down = to_y(cross, cross, 1, True)
     own.wait()
-    for copy in first_x:
-        copy.wait_recv()
-    row = out_ref.at[y, z, :, core]
-    second_y = [
-        send(row, row, y_send.at[NY - 1 + j], y_recv.at[NY - 1 + j], y_peers[j])
-        for j in range(NY - 1)
-    ]
-    to_core = [send(row, row, c_send.at[0], c_recv.at[0], partner)]
-    for copy in first_y:
-        copy.wait_recv()
-    column = out_ref.at[:, other, x, core]
-    second_x = [
-        send(column, column, x_send.at[NX - 1 + j], x_recv.at[NX - 1 + j], x_peers[j])
-        for j in range(NX - 1)
-    ]
-    to_core.append(send(column, column, c_send.at[1], c_recv.at[1], partner))
-    for j in range(NY - 1):
-        second_y[j].wait_recv()
-        far = out_ref.at[y_from[j], z, :, core]
-        to_core.append(send(far, far, c_send.at[2 + j], c_recv.at[2 + j], partner))
-    for j in range(NX - 1):
-        second_x[j].wait_recv()
-        far = out_ref.at[:, other, x_from[j], core]
-        slot = 1 + NY + j
-        to_core.append(send(far, far, c_send.at[slot], c_recv.at[slot], partner))
+    behind.wait_recv()
+    relay_x.wait_recv()
+    row_up = to_y(row(y), row(y), 3)
+    row_down = to_y(row(y), row(y), 4, True)
+    across(row(y))
+    up.wait_recv()
+    passed = out_ref.at[y_last, other, x, core]
+    relay_y = to_y(passed, passed, 2)
+    down.wait_recv()
+    relay_y.wait_recv()
+    column_up = to_x(column(x), column(x), 3)
+    column_down = to_x(column(x), column(x), 4, True)
+    across(column(x))
+    row_up.wait_recv()
+    row_relay = to_y(row(y_last), row(y_last), 5)
+    across(row(y_last))
+    row_down.wait_recv()
+    across(row(y_next))
+    column_up.wait_recv()
+    column_relay = to_x(column(x_last), column(x_last), 5)
+    across(column(x_last))
+    column_down.wait_recv()
+    across(column(x_next))
+    row_relay.wait_recv()
+    across(row(y_far))
+    column_relay.wait_recv()
+    across(column(x_far))
     for copy in to_core:
         copy.wait_recv()
-    for copy in [to_z] + first_x + first_y + second_y + second_x + to_core:
+    for copy in [to_z] + everything + to_core:
         copy.wait_send()
 
 

time: 95.1 us -> 95.2 us (level)
  the two profiles are of different devices: /device:TPU:25 before, /device:TPU:5 now
where the time goes in v4:
time: 95.2 us; the launch traced here: 94.9 us
  Pallas kernels  71.7 us (75%)
  matrix products  12.9 us (14%)
  local copies, waits for them, and re-layouts  5.95 us (6%)
  other arithmetic  3.38 us (4%)
  between operations  0.99 us (1%)
    pallas_call x1, Pallas kernels, gather(): pl.pallas_call(gather_kernel, out_shape=jax.ShapeDtypeStruct((NY, NZ, NX,...  37 us
    pallas_call x1, Pallas kernels, reduce(): pl.pallas_call(reduce_kernel, out_shape=(jax.ShapeDtypeStruct((groups, ha...  34.7 us
    dot_general x1, matrix products, local(): jnp.einsum('pm,pcn->mcn', class_hot, weighted, preferred_element_type=jnp...  6.04 us
    dot_general x1, matrix products, local(): ctf = jnp.dot(group_hot, ctf_local, preferred_element_type=jnp.float32)  2.33 us
    unnamed x8, local copies, waits for them, and re-layouts  2.07 us

profile of v4, /device:TPU:5, one launch (start us, length us, event | category | flops | bytes accessed | tf_op | source)
XLA Modules:
  0.0 94.9 jit_solution(12197014345557330745)
XLA Ops:
  0.0 0.7 multiply_add_fusion
  0.7 1.3 %fusion.29 = (bf16[128,16]{0,1:T(8,128)(2,1)S(1)}, bf16[128,16]{0,1:T(8,128)(2,1)S(1)}, bf16[128,16]{0,1:T(8,128)(2,1)S(1)}) fusion(s32[1024]{0:T(1024)} %param.10, s32[1024]{0:T(1024)S(1)} %multiply_add_fusion), kind=kOutput, calls=%fused_computation.63 | convolution fusion | flops 4431872 | bytes 20480 | tf_op jit(solution)/shard_map/pm,pg->mg/dot_general | solution.py:300
  2.0 2.3 %fusion.16 = f32[1024,2064]{0,1:T(8,128)S(1)} fusion(s32[1024]{0:T(1024)} %param.10, bf16[16,16512]{1,0:T(8,128)(2,1)} %param.12, s32[]{:T(128)S(6)} %select_n.22), kind=kOutput, calls=%fused_computation.22 | convolution fusion | flops 67649536 | bytes 8527876 | tf_op jit(solution)/shard_map/dot_general | solution.py:297
  4.3 6.0 %fusion.6 = bf16[128,2,2064]{0,2,1:T(8,128)(2,1)S(1)} fusion(bf16[1024,2,2064]{0,2,1:T(8,128)(2,1)} %param.7, f32[1024,2064]{0,1:T(8,128)S(1)} %fusion.16, s32[1024]{0:T(1024)S(1)} %multiply_add_fusion), kind=kOutput, calls=%fused_computation.8 | convolution fusion | flops 1095471104 | bytes 17969152 | tf_op jit(solution)/shard_map/pm,pcn->mcn/dot_general | solution.py:299
  10.4 0.1 fusion.9
  10.5 0.0 copy-start.1
  10.5 1.8 %copy.10 = bf16[128,2,2176]{2,1,0:T(2,128)(2,1)S(1)} copy(bf16[128,2,2176]{0,2,1:T(8,128)(2,1)S(1)} %fusion.9) | data formatting | bytes 2228224 | tf_op jit(solution)/shard_map/concatenate | solution.py:307
  12.4 0.5 reshape_reshape.3.message_ref
  12.8 34.7 %shard_map.73 = (f32[8,4,2176]{2,1,0:T(4,128)S(1)}, s32[32,8,128]{2,1,0:T(8,128)S(1)}) custom-call(bf16[4,2,4,8,2176]{4,3,2,1,0:T(8,128)(2,1)S(1)} %reshape_reshape.3.message_ref, s32[8,128]{1,0:T(8,128)S(1)} %pad_bitcast_fusion.cycles_ref), custom_call_target="tpu_custom_call" | custom-call | tf_op jit(solution)/shard_map/pallas_call | solution.py:245
  47.5 0.1 slice.57
  47.6 0.1 reshape_squeeze.3
  47.7 0.2 fusion.10
  48.0 0.2 reshape.57
  48.2 0.3 reduce_sum.72
  48.5 0.1 broadcast_add_fusion
  48.6 0.4 reshape.58
  49.0 0.1 broadcast_divide_fusion
  49.1 0.5 multiply_reduce_fusion.2
  49.8 0.2 fusion.28
  50.0 0.1 div.72
  50.1 0.3 fusion.25
  50.4 0.1 stack.18
  50.5 0.4 reduce-precision_convert_fusion.1
  50.9 0.1 eq.51
  51.1 1.5 %fusion.2 = f32[12,128]{1,0:T(8,128)S(1)} fusion(s32[16512]{0:T(1024)S(1)} %eq.51, bf16[4,16512]{1,0:T(4,128)(2,1)S(1)} %get-tuple-element.20, bf16[4,16512]{1,0:T(4,128)(2,1)S(1)} %get-tuple-element.19, bf16[4,16512]{1,0:T(4,128)(2,1)S(1)} %get-tuple-element.18), kind=kOutput, calls=%fused_computation.4 | convolution fusion | flops 54027264 | bytes 468480 | tf_op jit(solution)/shard_map/sn,rn->sr/dot_general | solution.py:337
  52.6 0.1 reduce_sum.77
  52.7 0.6 fusion.55
  54.0 1.5 %fusion.8 = f32[16512]{0:T(1024)S(1)} fusion(s32[16512]{0:T(1024)S(1)} %eq.51, bf16[1,128]{1,0:T(2,128)(2,1)S(1)} %get-tuple-element.28, bf16[1,128]{1,0:T(2,128)(2,1)S(1)} %get-tuple-element.27, bf16[1,128]{1,0:T(2,128)(2,1)S(1)} %get-tuple-element.12), kind=kOutput, calls=%fused_computation.11 | convolution fusion | flops 14830080 | bytes 132864 | tf_op jit(solution)/shard_map/dot_general | solution.py:344
  55.5 0.2 add.75
  55.7 0.1 multiply_convert_fusion.6.unit_ref
  55.8 37.0 %shard_map.74 = bf16[4,2,4,2,2,16512]{5,4,3,2,1,0:T(2,128)(2,1)S(1)} custom-call(bf16[2,16512]{1,0:T(2,128)(2,1)S(1)} %multiply_convert_fusion.6.unit_ref), custom_call_target="tpu_custom_call" | custom-call | tf_op jit(solution)/shard_map/pallas_call | solution.py:129
  92.9 2.0 %copy.17 = bf16[64,2,16512]{2,1,0:T(2,128)(2,1)} copy(bf16[64,2,16512]{2,1,0:T(2,128)(2,1)S(1)} %bitcast.48) | data formatting | bytes 8454144
  (20 shorter events, 0.3 us)
Async XLA Ops:
  10.5 2.4 %copy-start.1 = (s32[516]{0:T(1024)S(1)}, s32[516]{0:T(1024)}, u32[]{:S(2)}) copy-start(s32[516]{0:T(1024)} %param.11) | copy-start | bytes 6196
  12.3 35.4 %copy-start = (bf16[16,16512]{1,0:T(8,128)(2,1)S(1)}, bf16[16,16512]{1,0:T(8,128)(2,1)}, u32[]{:S(2)}) copy-start(bf16[16,16512]{1,0:T(8,128)(2,1)} %param.12) | copy-start | bytes 1585156
  50.9 1.8 %copy-start.2 = (f32[128]{0:T(128)S(1)}, f32[128]{0:T(128)}, u32[]{:S(2)}) copy-start(f32[128]{0:T(128)} %param.13) | copy-start | bytes 1540

commit v5 on v4

--- a/solution.py
+++ b/solution.py
@@ -30,16 +30,19 @@
         return ((yy * NZ + zz) * NX + xx, cls)
 
     partner = (dom, cls + 1 - 2 * core)
-    z_peer = at(y, other, x)
+    mirrored = lax.axis_size("cls") - NC - (cls - core) + core
+    z_peer = (at(y, other, x)[0], mirrored)
     turn = 1 - 2 * core
     x_next, x_last = lax.rem(x + turn + NX, NX), lax.rem(x - turn + NX, NX)
     y_next, y_last = lax.rem(y + turn + NY, NY), lax.rem(y - turn + NY, NY)
     x_far, y_far = lax.rem(x + 2, NX), lax.rem(y + 2, NY)
     x_peers = [at(y, z, x_next), at(y, z, x_last)]
     y_peers = [at(y_next, z, x), at(y_last, z, x)]
+    x_partner = (at(y, z, x_last)[0], partner[1])
+    y_partner = (at(y_last, z, x)[0], partner[1])
 
     barrier = pltpu.get_barrier_semaphore()
-    everyone = [partner, z_peer] + x_peers + y_peers
+    everyone = [partner, z_peer, x_partner, y_partner] + x_peers + y_peers
     for peer in everyone:
         pl.semaphore_signal(barrier, inc=1, device_id=peer, device_id_type=MESH)
     pl.semaphore_wait(barrier, len(everyone))
@@ -66,9 +69,9 @@
 
     to_core = []
 
-    def across(ref):
+    def across(ref, peer=partner):
         slot = len(to_core)
-        to_core.append(send(ref, ref, c_send.at[slot], c_recv.at[slot], partner))
+        to_core.append(send(ref, ref, c_send.at[slot], c_recv.at[slot], peer))
 
     def row(yy):
         return out_ref.at[yy, z, :, core]
@@ -95,6 +98,7 @@
     row_up = to_y(row(y), row(y), 3)
     row_down = to_y(row(y), row(y), 4, True)
     across(row(y))
+    across(row(y), y_partner)
     up.wait_recv()
     passed = out_ref.at[y_last, other, x, core]
     relay_y = to_y(passed, passed, 2)
@@ -103,16 +107,15 @@
     column_up = to_x(column(x), column(x), 3)
     column_down = to_x(column(x), column(x), 4, True)
     across(column(x))
+    across(column(x), x_partner)
     row_up.wait_recv()
     row_relay = to_y(row(y_last), row(y_last), 5)
     across(row(y_last))
     row_down.wait_recv()
-    across(row(y_next))
     column_up.wait_recv()
     column_relay = to_x(column(x_last), column(x_last), 5)
     across(column(x_last))
     column_down.wait_recv()
-    across(column(x_next))
     row_relay.wait_recv()
     across(row(y_far))
     column_relay.wait_recv()

time: 95.2 us -> 97.3 us (1.022)
  the two profiles are of different devices: /device:TPU:5 before, /device:TPU:1 now
where the time goes in v5:
time: 97.3 us; the launch traced here: 97 us
  Pallas kernels  73.8 us (76%)
  matrix products  12.9 us (13%)
  local copies, waits for them, and re-layouts  5.95 us (6%)
  other arithmetic  3.38 us (3%)
  between operations  0.99 us (1%)
    pallas_call x1, Pallas kernels, gather(): pl.pallas_call(gather_kernel, out_shape=jax.ShapeDtypeStruct((NY, NZ, NX,...  37.8 us
    pallas_call x1, Pallas kernels, reduce(): pl.pallas_call(reduce_kernel, out_shape=(jax.ShapeDtypeStruct((groups, ha...  36.1 us
    dot_general x1, matrix products, local(): jnp.einsum('pm,pcn->mcn', class_hot, weighted, preferred_element_type=jnp...  6.04 us
    dot_general x1, matrix products, local(): ctf = jnp.dot(group_hot, ctf_local, preferred_element_type=jnp.float32)  2.33 us
    unnamed x8, local copies, waits for them, and re-layouts  2.07 us

profile of v5, /device:TPU:1, one launch (start us, length us, event | category | flops | bytes accessed | tf_op | source)
XLA Modules:
  0.0 97.0 jit_solution(16510566688893768165)
XLA Ops:
  0.0 0.7 multiply_add_fusion
  0.7 1.3 %fusion.29 = (bf16[128,16]{0,1:T(8,128)(2,1)S(1)}, bf16[128,16]{0,1:T(8,128)(2,1)S(1)}, bf16[128,16]{0,1:T(8,128)(2,1)S(1)}) fusion(s32[1024]{0:T(1024)} %param.10, s32[1024]{0:T(1024)S(1)} %multiply_add_fusion), kind=kOutput, calls=%fused_computation.63 | convolution fusion | flops 4431872 | bytes 20480 | tf_op jit(solution)/shard_map/pm,pg->mg/dot_general | solution.py:303
  2.0 2.3 %fusion.16 = f32[1024,2064]{0,1:T(8,128)S(1)} fusion(s32[1024]{0:T(1024)} %param.10, bf16[16,16512]{1,0:T(8,128)(2,1)} %param.12, s32[]{:T(128)S(6)} %select_n.22), kind=kOutput, calls=%fused_computation.22 | convolution fusion | flops 67649536 | bytes 8527876 | tf_op jit(solution)/shard_map/dot_general | solution.py:300
  4.3 6.0 %fusion.6 = bf16[128,2,2064]{0,2,1:T(8,128)(2,1)S(1)} fusion(bf16[1024,2,2064]{0,2,1:T(8,128)(2,1)} %param.7, f32[1024,2064]{0,1:T(8,128)S(1)} %fusion.16, s32[1024]{0:T(1024)S(1)} %multiply_add_fusion), kind=kOutput, calls=%fused_computation.8 | convolution fusion | flops 1095471104 | bytes 17969152 | tf_op jit(solution)/shard_map/pm,pcn->mcn/dot_general | solution.py:302
  10.4 0.1 fusion.9
  10.5 0.0 copy-start.1
  10.5 1.8 %copy.10 = bf16[128,2,2176]{2,1,0:T(2,128)(2,1)S(1)} copy(bf16[128,2,2176]{0,2,1:T(8,128)(2,1)S(1)} %fusion.9) | data formatting | bytes 2228224 | tf_op jit(solution)/shard_map/concatenate | solution.py:310
  12.4 0.5 reshape_reshape.3.message_ref
  12.8 36.1 %shard_map.73 = (f32[8,4,2176]{2,1,0:T(4,128)S(1)}, s32[32,8,128]{2,1,0:T(8,128)S(1)}) custom-call(bf16[4,2,4,8,2176]{4,3,2,1,0:T(8,128)(2,1)S(1)} %reshape_reshape.3.message_ref, s32[8,128]{1,0:T(8,128)S(1)} %pad_bitcast_fusion.cycles_ref), custom_call_target="tpu_custom_call" | custom-call | tf_op jit(solution)/shard_map/pallas_call | solution.py:248
  48.9 0.1 slice.57
  49.0 0.1 reshape_squeeze.3
  49.1 0.2 fusion.10
  49.3 0.2 reshape.57
  49.6 0.3 reduce_sum.72
  49.8 0.1 broadcast_add_fusion
  50.0 0.4 reshape.58
  50.3 0.1 broadcast_divide_fusion
  50.5 0.5 multiply_reduce_fusion.2
  51.2 0.2 fusion.28
  51.4 0.1 div.72
  51.5 0.3 fusion.25
  51.8 0.1 stack.18
  51.9 0.4 reduce-precision_convert_fusion.1
  52.3 0.1 eq.51
  52.5 1.5 %fusion.2 = f32[12,128]{1,0:T(8,128)S(1)} fusion(s32[16512]{0:T(1024)S(1)} %eq.51, bf16[4,16512]{1,0:T(4,128)(2,1)S(1)} %get-tuple-element.20, bf16[4,16512]{1,0:T(4,128)(2,1)S(1)} %get-tuple-element.19, bf16[4,16512]{1,0:T(4,128)(2,1)S(1)} %get-tuple-element.18), kind=kOutput, calls=%fused_computation.4 | convolution fusion | flops 54027264 | bytes 468480 | tf_op jit(solution)/shard_map/sn,rn->sr/dot_general | solution.py:340
  54.0 0.1 reduce_sum.77
  54.1 0.6 fusion.55
  55.4 1.5 %fusion.8 = f32[16512]{0:T(1024)S(1)} fusion(s32[16512]{0:T(1024)S(1)} %eq.51, bf16[1,128]{1,0:T(2,128)(2,1)S(1)} %get-tuple-element.28, bf16[1,128]{1,0:T(2,128)(2,1)S(1)} %get-tuple-element.27, bf16[1,128]{1,0:T(2,128)(2,1)S(1)} %get-tuple-element.12), kind=kOutput, calls=%fused_computation.11 | convolution fusion | flops 14830080 | bytes 132864 | tf_op jit(solution)/shard_map/dot_general | solution.py:347
  56.9 0.2 add.75
  57.1 0.1 multiply_convert_fusion.6.unit_ref
  57.2 37.8 %shard_map.74 = bf16[4,2,4,2,2,16512]{5,4,3,2,1,0:T(2,128)(2,1)S(1)} custom-call(bf16[2,16512]{1,0:T(2,128)(2,1)S(1)} %multiply_convert_fusion.6.unit_ref), custom_call_target="tpu_custom_call" | custom-call | tf_op jit(solution)/shard_map/pallas_call | solution.py:132
  95.0 2.0 %copy.17 = bf16[64,2,16512]{2,1,0:T(2,128)(2,1)} copy(bf16[64,2,16512]{2,1,0:T(2,128)(2,1)S(1)} %bitcast.48) | data formatting | bytes 8454144
  (20 shorter events, 0.3 us)
Async XLA Ops:
  10.5 2.4 %copy-start.1 = (s32[516]{0:T(1024)S(1)}, s32[516]{0:T(1024)}, u32[]{:S(2)}) copy-start(s32[516]{0:T(1024)} %param.11) | copy-start | bytes 6196
  12.3 36.8 %copy-start = (bf16[16,16512]{1,0:T(8,128)(2,1)S(1)}, bf16[16,16512]{1,0:T(8,128)(2,1)}, u32[]{:S(2)}) copy-start(bf16[16,16512]{1,0:T(8,128)(2,1)} %param.12) | copy-start | bytes 1585156
  52.3 1.8 %copy-start.2 = (f32[128]{0:T(128)S(1)}, f32[128]{0:T(128)}, u32[]{:S(2)}) copy-start(f32[128]{0:T(128)} %param.13) | copy-start | bytes 1540

commit v6 on v3

--- a/solution.py
+++ b/solution.py
@@ -30,7 +30,8 @@
         return ((yy * NZ + zz) * NX + xx, cls)
 
     partner = (dom, cls + 1 - 2 * core)
-    z_peer = at(y, other, x)
+    mirrored = lax.axis_size("cls") - NC - (cls - core) + core
+    z_peer = (at(y, other, x)[0], mirrored)
     x_peers = [at(y, z, lax.rem(x + j, NX)) for j in range(1, NX)]
     y_peers = [at(lax.rem(y + j, NY), z, x) for j in range(1, NY)]
     x_from = [lax.rem(x + NX - j, NX) for j in range(1, NX)]
@@ -157,7 +158,10 @@
     own_cycles = pltpu.make_async_copy(cycles_ref, cycles_out_ref.at[dom], own_sem.at[1])
     own_cycles.start()
     sends = []
-    for step in range(1, NY * NX):
+    far_first = sorted(
+        range(1, NY * NX), key=lambda step: -(step // NX == NY // 2) - (step % NX == NX // 2)
+    )
+    for step in far_first:
         yy, xx = plane[step]
         copy = pltpu.make_async_remote_copy(
             src_ref=message_ref.at[yy, :, xx], dst_ref=got.at[step],

time: 95.1 us -> 90.3 us (0.950)
  Pallas kernels: 71.7 us -> 66.9 us
    pallas_call x1, Pallas kernels: 36.9 us -> 32.5 us  [gather(): pl.pallas_call(gather_kernel, out_shape=jax.ShapeDtypeStruct((NY, NZ, NX,...]
where the time goes in v6:
time: 90.3 us; the launch traced here: 90 us
  Pallas kernels  66.9 us (74%)
  matrix products  12.9 us (14%)
  local copies, waits for them, and re-layouts  5.95 us (7%)
  other arithmetic  3.38 us (4%)
  between operations  0.99 us (1%)
    pallas_call x1, Pallas kernels, reduce(): pl.pallas_call(reduce_kernel, out_shape=(jax.ShapeDtypeStruct((groups, ha...  34.4 us
    pallas_call x1, Pallas kernels, gather(): pl.pallas_call(gather_kernel, out_shape=jax.ShapeDtypeStruct((NY, NZ, NX,...  32.5 us
    dot_general x1, matrix products, local(): jnp.einsum('pm,pcn->mcn', class_hot, weighted, preferred_element_type=jnp...  6.04 us
    dot_general x1, matrix products, local(): ctf = jnp.dot(group_hot, ctf_local, preferred_element_type=jnp.float32)  2.33 us
    unnamed x8, local copies, waits for them, and re-layouts  2.07 us
    concatenate x1, local copies, waits for them, and re-layouts, local(): jnp.concatenate([partial_sums.astype(jnp.bfloat16), digits.astype(jnp.bfl...  1.85 us

profile of v6, /device:TPU:25, one launch (start us, length us, event | category | flops | bytes accessed | tf_op | source)
XLA Modules:
  0.0 90.0 jit_solution(12277665743202954580)
XLA Ops:
  0.0 0.7 multiply_add_fusion
  0.7 1.3 %fusion.29 = (bf16[128,16]{0,1:T(8,128)(2,1)S(1)}, bf16[128,16]{0,1:T(8,128)(2,1)S(1)}, bf16[128,16]{0,1:T(8,128)(2,1)S(1)}) fusion(s32[1024]{0:T(1024)} %param.10, s32[1024]{0:T(1024)S(1)} %multiply_add_fusion), kind=kOutput, calls=%fused_computation.63 | convolution fusion | flops 4431872 | bytes 20480 | tf_op jit(solution)/shard_map/pm,pg->mg/dot_general | solution.py:273
  2.0 2.3 %fusion.16 = f32[1024,2064]{0,1:T(8,128)S(1)} fusion(s32[1024]{0:T(1024)} %param.10, bf16[16,16512]{1,0:T(8,128)(2,1)} %param.12, s32[]{:T(128)S(6)} %select_n.22), kind=kOutput, calls=%fused_computation.22 | convolution fusion | flops 67649536 | bytes 8527876 | tf_op jit(solution)/shard_map/dot_general | solution.py:270
  4.3 6.0 %fusion.6 = bf16[128,2,2064]{0,2,1:T(8,128)(2,1)S(1)} fusion(bf16[1024,2,2064]{0,2,1:T(8,128)(2,1)} %param.7, f32[1024,2064]{0,1:T(8,128)S(1)} %fusion.16, s32[1024]{0:T(1024)S(1)} %multiply_add_fusion), kind=kOutput, calls=%fused_computation.8 | convolution fusion | flops 1095471104 | bytes 17969152 | tf_op jit(solution)/shard_map/pm,pcn->mcn/dot_general | solution.py:272
  10.4 0.1 fusion.9
  10.5 0.0 copy-start.1
  10.5 1.8 %copy.10 = bf16[128,2,2176]{2,1,0:T(2,128)(2,1)S(1)} copy(bf16[128,2,2176]{0,2,1:T(8,128)(2,1)S(1)} %fusion.9) | data formatting | bytes 2228224 | tf_op jit(solution)/shard_map/concatenate | solution.py:280
  12.4 0.5 reshape_reshape.3.message_ref
  12.8 34.4 %shard_map.73 = (f32[8,4,2176]{2,1,0:T(4,128)S(1)}, s32[32,8,128]{2,1,0:T(8,128)S(1)}) custom-call(bf16[4,2,4,8,2176]{4,3,2,1,0:T(8,128)(2,1)S(1)} %reshape_reshape.3.message_ref, s32[8,128]{1,0:T(8,128)S(1)} %pad_bitcast_fusion.cycles_ref), custom_call_target="tpu_custom_call" | custom-call | tf_op jit(solution)/shard_map/pallas_call | solution.py:218
  47.3 0.1 slice.57
  47.4 0.1 reshape_squeeze.3
  47.5 0.2 fusion.10
  47.7 0.2 reshape.57
  47.9 0.3 reduce_sum.72
  48.2 0.1 broadcast_add_fusion
  48.3 0.4 reshape.58
  48.7 0.1 broadcast_divide_fusion
  48.8 0.5 multiply_reduce_fusion.2
  49.5 0.2 fusion.28
  49.7 0.1 div.72
  49.8 0.3 fusion.25
  50.1 0.1 stack.18
  50.2 0.4 reduce-precision_convert_fusion.1
  50.7 0.1 eq.51
  50.8 1.5 %fusion.2 = f32[12,128]{1,0:T(8,128)S(1)} fusion(s32[16512]{0:T(1024)S(1)} %eq.51, bf16[4,16512]{1,0:T(4,128)(2,1)S(1)} %get-tuple-element.20, bf16[4,16512]{1,0:T(4,128)(2,1)S(1)} %get-tuple-element.19, bf16[4,16512]{1,0:T(4,128)(2,1)S(1)} %get-tuple-element.18), kind=kOutput, calls=%fused_computation.4 | convolution fusion | flops 54027264 | bytes 468480 | tf_op jit(solution)/shard_map/sn,rn->sr/dot_general | solution.py:310
  52.3 0.1 reduce_sum.77
  52.4 0.6 fusion.55
  53.8 1.5 %fusion.8 = f32[16512]{0:T(1024)S(1)} fusion(s32[16512]{0:T(1024)S(1)} %eq.51, bf16[1,128]{1,0:T(2,128)(2,1)S(1)} %get-tuple-element.28, bf16[1,128]{1,0:T(2,128)(2,1)S(1)} %get-tuple-element.27, bf16[1,128]{1,0:T(2,128)(2,1)S(1)} %get-tuple-element.12), kind=kOutput, calls=%fused_computation.11 | convolution fusion | flops 14830080 | bytes 132864 | tf_op jit(solution)/shard_map/dot_general | solution.py:317
  55.2 0.2 add.75
  55.4 0.1 multiply_convert_fusion.6.unit_ref
  55.6 32.5 %shard_map.74 = bf16[4,2,4,2,2,16512]{5,4,3,2,1,0:T(2,128)(2,1)S(1)} custom-call(bf16[2,16512]{1,0:T(2,128)(2,1)S(1)} %multiply_convert_fusion.6.unit_ref), custom_call_target="tpu_custom_call" | custom-call | tf_op jit(solution)/shard_map/pallas_call | solution.py:99
  88.0 2.0 %copy.17 = bf16[64,2,16512]{2,1,0:T(2,128)(2,1)} copy(bf16[64,2,16512]{2,1,0:T(2,128)(2,1)S(1)} %bitcast.48) | data formatting | bytes 8454144
  (20 shorter events, 0.3 us)
Async XLA Ops:
  10.5 2.4 %copy-start.1 = (s32[516]{0:T(1024)S(1)}, s32[516]{0:T(1024)}, u32[]{:S(2)}) copy-start(s32[516]{0:T(1024)} %param.11) | copy-start | bytes 6196
  12.3 35.1 %copy-start = (bf16[16,16512]{1,0:T(8,128)(2,1)S(1)}, bf16[16,16512]{1,0:T(8,128)(2,1)}, u32[]{:S(2)}) copy-start(bf16[16,16512]{1,0:T(8,128)(2,1)} %param.12) | copy-start | bytes 1585156
  50.6 1.8 %copy-start.2 = (f32[128]{0:T(128)S(1)}, f32[128]{0:T(128)}, u32[]{:S(2)}) copy-start(f32[128]{0:T(128)} %param.13) | copy-start | bytes 1540
